TPU v7x, 256 devices: a whole 4x4x8 slice. The times are simulated.
256 devices in a mesh: wide: 16 (over z_hi, x, core), col: 16 (over y, z_lo).
Axes of the slice: x: 4, y: 4, z: 8 (z_hi: 2, z_lo: 4; z = z_hi * 4 + z_lo), core: 2. Of those that a mesh axis runs over, the one named last changes fastest.
Arguments:
- adjoint: bfloat16 [32, 6144], P(None, ('wide', 'col')), may hold values from -6 to 6
- operator: bfloat16 [6144, 196608], P('wide', 'col'), may hold values from -0.109375 to 0.109375
- owner: int32 [196608], P(('col', 'wide')), may hold values from 0 to 196607, as said below
Outputs:
- junction_sums: float32 [32, 196608], P(None, ('col', 'wide'))
Inputs may be any that keep to these rules, and one draw needn't show every extreme that they name: Unknown j of device block b = j // 768 (blocks ordered col first, then wide) has owner j itself, or is a duplicate whose owner is an unknown in the lower half of a block of the same index of col; duplicates lie only in the upper half of a block and owners of duplicates are never duplicates. One block hands at most 16 duplicates to the blocks of any one index of wide, and this count is reached in every draw, by some block towards every index of wide and towards some index of wide from every block.
All inputs are finite; a program needn't handle non-finite values.
Results may differ from a plain program's by a relative error of at most 0.0003.
Values may be sent and summed in bfloat16 or wider, within the bound.
No kernel may reach another device: no remote copies, remote signals or barrier semaphores. Data moves between devices by JAX's collectives and lax.ppermute only.
A program may use at most 64 MiB of HBM per device.

v0:
```python
import jax
import jax.numpy as jnp
from jax import lax
from jax.sharding import PartitionSpec as P

CAP = 16


def local(adjoint, operator, owner):
    wide_count = lax.axis_size("wide")
    own_width = owner.shape[0]
    block_cols = operator.shape[1]
    sensors = adjoint.shape[0]
    partials = jnp.dot(
        lax.all_gather(adjoint, "col", axis=1, tiled=True),
        operator,
        preferred_element_type=jnp.float32,
    )
    col_base = lax.axis_index("col") * block_cols
    summed = lax.psum_scatter(partials, "wide", scatter_dimension=1, tiled=True)
    positions = jnp.arange(own_width, dtype=jnp.int32)
    global_cols = col_base + lax.axis_index("wide") * own_width + positions
    repeated = owner != global_cols
    target_peer = owner // own_width % wide_count
    target_place = owner % own_width
    peers = jnp.arange(wide_count, dtype=jnp.int32)
    marks = ((target_peer[:, None] == peers[None, :]) & repeated[:, None]).astype(jnp.int32)
    ranking = jnp.sum((jnp.cumsum(marks, axis=0) - marks) * marks, axis=1)
    slot_of = target_peer * CAP + ranking
    slot_ids = jnp.arange(wide_count * CAP, dtype=jnp.int32)
    chosen = (slot_of[:, None] == slot_ids[None, :]) & repeated[:, None]
    selector = chosen.astype(jnp.float32)
    outgoing = jnp.dot(
        summed, selector, precision=lax.Precision.HIGHEST, preferred_element_type=jnp.float32
    )
    place_sum = jnp.sum(chosen.astype(jnp.int32) * (target_place + 1)[:, None], axis=0) - 1
    outgoing = outgoing.reshape(sensors, wide_count, CAP)
    places = place_sum.astype(jnp.float32).reshape(1, wide_count, CAP)
    arrived, arrived_places = (
        lax.all_to_all(outgoing, "wide", split_axis=1, concat_axis=1, tiled=True),
        lax.all_to_all(places, "wide", split_axis=1, concat_axis=1, tiled=True),
    )
    flat_values = arrived.reshape(sensors, wide_count * CAP)
    landing = arrived_places.reshape(-1).astype(jnp.int32)
    receiver = (landing[:, None] == positions[None, :]).astype(jnp.float32)
    kept = summed * (1.0 - repeated.astype(jnp.float32))[None, :]
    added = jnp.dot(
        flat_values, receiver, precision=lax.Precision.HIGHEST, preferred_element_type=jnp.float32
    )
    return kept + added


def solution(mesh):
    return jax.shard_map(
        local,
        mesh=mesh,
        in_specs=(P(None, ("wide", "col")), P("wide", "col"), P(("col", "wide"))),
        out_specs=P(None, ("col", "wide")),
        check_vma=False,
    )
```

profile of v0, /device:TPU:1, one launch (start us, length us, event | category | flops | bytes accessed | tf_op | source)
XLA Modules:
  0.0 167.5 jit_solution(11518465624353053526)
XLA Ops:
  6.5 0.0 copy-start
  6.5 0.0 reduce-scatter.2.cloned.1.call-start
  6.5 38.5 %all_gather.3 = bf16[32,384]{0,1:T(8,128)(2,1)S(1)} all-gather(bf16[32,24]{0,1:T(8,128)(2,1)} %param.3), channel_id=1, replica_groups=mesh['wide'=16,'col'=16] {'col'}, dimensions={1}, use_global_device_ids=true | all-gather | bytes 26112 | tf_op jit(solution)/shard_map/all_gather | solution.py:15
  45.0 6.5 %fusion.15 = f32[32,12288]{1,0:T(8,128)} fusion(bf16[32,384]{0,1:T(8,128)(2,1)S(1)} %all_gather.3, bf16[384,12288]{1,0:T(8,128)(2,1)} %param.4), kind=kOutput, calls=%fused_computation.35 | convolution fusion | flops 301989888 | bytes 11034624 | tf_op jit(solution)/shard_map/dot_general | solution.py:14
  51.5 0.0 reduce-scatter.2.cloned.1.call-update
  51.5 0.0 copy-done
  51.6 1.7 %reduce-window.6 = s32[16,6,128]{2,0,1:T(8,128)S(1)} reduce-window(s32[16,6,128]{2,0,1:T(8,128)S(1)} %fusion.11, s32[]{:T(128)} %constant.48.clone.1), window={size=1x1x128 pad=0_0x0_0x127_0}, to_apply=%region_1.2 | reduce-window | flops 1560576 | bytes 98308 | tf_op jit(solution)/shard_map/reduce-window
  53.3 0.3 slice_reduce_fusion
  53.6 0.1 fusion.8
  53.7 0.7 select_reduce_fusion
  54.4 0.7 convert_element_type.40
  55.1 16.2 %all-to-all-start.1 = ((f32[1,16,16]{2,0,1:T(1,128)}), f32[1,16,16]{2,0,1:T(1,128)S(1)}, u32[]{:S(2)}, u32[]{:S(2)}) async-start(f32[1,16,16]{2,0,1:T(1,128)} %convert_element_type.40), calls=%async_computation.2 | async-start | bytes 16384 | tf_op jit(solution)/shard_map/all_to_all | solution.py:41
  71.2 67.5 %reduce-scatter.2.cloned.1.call-done = f32[32,768]{1,0:T(8,128)} async-done(((f32[32,12288]{1,0:T(8,128)}), f32[32,768]{1,0:T(8,128)}) %reduce-scatter.2.cloned.1.call-update) | async-done | bytes 98320 | tf_op jit(solution)/shard_map/reduce_scatter | solution.py:20
  138.8 1.9 %fusion.1 = f32[32,256]{0,1:T(8,128)S(1)} fusion(f32[32,768]{1,0:T(8,128)} %reduce-scatter.2.cloned.1.call-done, s32[768]{0:T(1024)S(1)} %multiply_add_fusion, pred[768]{0:T(1024)(128)(4,1)S(1)} %get-tuple-element.6), kind=kOutput, calls=%fused_computation.5 | convolution fusion | flops 75890688 | bytes 134912 | tf_op jit(solution)/shard_map/dot_general | solution.py:33
  140.7 0.7 reshape.65
  141.4 0.0 all-to-all-done.1
  141.4 6.2 %all-to-all-start = ((f32[16,1,512]{2,1,0:T(1,128)}), f32[16,1,512]{2,1,0:T(1,128)S(1)}, u32[]{:S(2)}, u32[]{:S(2)}) async-start(f32[16,1,512]{2,1,0:T(1,128)} %reshape.65), calls=%async_computation.1 | async-start | bytes 65536 | tf_op jit(solution)/shard_map/all_to_all | solution.py:40
  147.6 0.1 convert_element_type.42
  147.7 9.6 %all-to-all-done = f32[16,1,512]{2,1,0:T(1,128)S(1)} async-done(((f32[16,1,512]{2,1,0:T(1,128)}), f32[16,1,512]{2,1,0:T(1,128)S(1)}, u32[]{:S(2)}, u32[]{:S(2)}) %all-to-all-start) | async-done | bytes 32800 | tf_op jit(solution)/shard_map/all_to_all | solution.py:40
  157.3 0.5 broadcast.60
  157.8 0.7 reduce.6
  158.6 0.1 reshape.66
  158.6 2.0 %convolution_add_fusion = f32[32,768]{1,0:T(8,128)} fusion(f32[32,256]{0,1:T(8,128)S(1)} %bitcast.30, s32[256]{0:T(256)S(1)} %convert_element_type.42, f32[32,768]{1,0:T(8,128)} %reduce-scatter.2.cloned.1.call-done, f32[768]{0:T(1024)S(1)} %get-tuple-element.5), kind=kOutput, calls=%fused_computation | convolution fusion | flops 75743232 | bytes 233472 | tf_op jit(solution)/shard_map/dot_general | solution.py:47
  (7 shorter events, 0.1 us)
Async XLA Ops:
  6.5 45.0 %copy-start = (s32[768]{0:T(1024)S(1)}, s32[768]{0:T(1024)}, u32[]{:S(2)}) copy-start(s32[768]{0:T(1024)} %param.5) | copy-start | bytes 9220
  6.5 132.2 %reduce-scatter.2.cloned.1.call-start = ((), (), s32[]{:S(2)}) async-start(), calls=%async_computation.3 | async-start | bytes 1671168 | tf_op jit(solution)/shard_map/reduce_scatter | solution.py:20
  55.1 86.3 %all-to-all-start.1 = ((f32[1,16,16]{2,0,1:T(1,128)}), f32[1,16,16]{2,0,1:T(1,128)S(1)}, u32[]{:S(2)}, u32[]{:S(2)}) async-start(f32[1,16,16]{2,0,1:T(1,128)} %convert_element_type.40), calls=%async_computation.2 | async-start | bytes 16384 | tf_op jit(solution)/shard_map/all_to_all | solution.py:41
  141.4 15.9 %all-to-all-start = ((f32[16,1,512]{2,1,0:T(1,128)}), f32[16,1,512]{2,1,0:T(1,128)S(1)}, u32[]{:S(2)}, u32[]{:S(2)}) async-start(f32[16,1,512]{2,1,0:T(1,128)} %reshape.65), calls=%async_computation.1 | async-start | bytes 65536 | tf_op jit(solution)/shard_map/all_to_all | solution.py:40
Sparse Core Ops, SparseCore 0:
  51.6 87.0 reduce-scatter.1
where the time goes:
time: 168 us; the launch traced here: 167 us
  waiting for transfers between devices  77.2 us (46%)
  blocking collectives  38.5 us (23%)
  starting transfers between devices  22.3 us (13%)
  between operations  13.5 us (8%)
  matrix products  10.4 us (6%)
  other arithmetic  3.3 us (2%)
  local copies, waits for them, and re-layouts  2.36 us (1%)
    reduce_scatter x1, waiting for transfers between devices, local(): summed = lax.psum_scatter(partials, 'wide', scatter_dimension=1, tiled=True)  67.5 us
    all_gather x1, blocking collectives, local(): lax.all_gather(adjoint, 'col', axis=1, tiled=True)  38.5 us
    all_to_all x1, starting transfers between devices, local(): lax.all_to_all(places, 'wide', split_axis=1, concat_axis=1, tiled=True)  16.2 us
    all_to_all x1, waiting for transfers between devices, local(): lax.all_to_all(outgoing, 'wide', split_axis=1, concat_axis=1, tiled=True)  9.6 us
    dot_general x1, matrix products, local(): jnp.dot(lax.all_gather(adjoint, 'col', axis=1, tiled=True), operator, pre...  6.5 us
    all_to_all x1, starting transfers between devices, local(): lax.all_to_all(outgoing, 'wide', split_axis=1, concat_axis=1, tiled=True)  6.19 us
  transfers between devices with their start and end apart: 3, of which 2 were waited for; matrix products, arithmetic and copies ran while one was open for 4% of the time, Pallas kernels for 0%

commit v1 on v0

--- a/solution.py
+++ b/solution.py
@@ -1,9 +1,20 @@
+import functools
 import jax
 import jax.numpy as jnp
 from jax import lax
 from jax.sharding import PartitionSpec as P
+from jax.lax import all_to_all, axis_size
 
 CAP = 16
+
+
+def report_plane_all(local_array, along_axis, d_out):
+    met_up = all_to_all(jnp.stack(axis_size(along_axis) * [local_array]), along_axis, 0, 0)
+    out_arr = jnp.concatenate(met_up, axis=d_out)
+    return out_arr
+
+
+tell_patches = functools.partial(report_plane_all, along_axis="col", d_out=1)
 
 
 def local(adjoint, operator, owner):
@@ -11,11 +22,7 @@
     own_width = owner.shape[0]
     block_cols = operator.shape[1]
     sensors = adjoint.shape[0]
-    partials = jnp.dot(
-        lax.all_gather(adjoint, "col", axis=1, tiled=True),
-        operator,
-        preferred_element_type=jnp.float32,
-    )
+    partials = jnp.dot(tell_patches(adjoint), operator, preferred_element_type=jnp.float32)
     col_base = lax.axis_index("col") * block_cols
     summed = lax.psum_scatter(partials, "wide", scatter_dimension=1, tiled=True)
     positions = jnp.arange(own_width, dtype=jnp.int32)

time: 168 us -> 141 us (0.84)
  blocking collectives: 38.5 us -> 15.8 us
  starting transfers between devices: 22.3 us -> 16.5 us
    all_gather x1 -> x0, blocking collectives: 38.5 us -> none  [local(): lax.all_gather(adjoint, 'col', axis=1, tiled=True)]
    all_to_all x0 -> x1, blocking collectives: none -> 15.8 us  [report_plane_all(): all_to_all(jnp.stack(axis_size(along_axis) * [local_array]), along_axis,...]
    all_to_all x1, starting transfers between devices: 16.2 us -> 10.3 us  [local(): lax.all_to_all(places, 'wide', split_axis=1, concat_axis=1, tiled=True)]
where the time goes in v1:
time: 141 us
  waiting for transfers between devices  77.8 us (55%)
  starting transfers between devices  16.5 us (12%)
  blocking collectives  15.8 us (11%)
  between operations  13.5 us (10%)
  matrix products  10.4 us (7%)
  local copies, waits for them, and re-layouts  3.3 us (2%)
  other arithmetic  3.3 us (2%)
    reduce_scatter x1, waiting for transfers between devices, local(): summed = lax.psum_scatter(partials, 'wide', scatter_dimension=1, tiled=True)  68.2 us
    all_to_all x1, blocking collectives, report_plane_all(): all_to_all(jnp.stack(axis_size(along_axis) * [local_array]), along_axis,...  15.8 us
    all_to_all x1, starting transfers between devices, local(): lax.all_to_all(places, 'wide', split_axis=1, concat_axis=1, tiled=True)  10.3 us
    all_to_all x1, waiting for transfers between devices, local(): lax.all_to_all(outgoing, 'wide', split_axis=1, concat_axis=1, tiled=True)  9.6 us
    dot_general x1, matrix products, local(): jnp.dot(tell_patches(adjoint), operator, preferred_element_type=jnp.float32)  6.5 us
    all_to_all x1, starting transfers between devices, local(): lax.all_to_all(outgoing, 'wide', split_axis=1, concat_axis=1, tiled=True)  6.15 us
  transfers between devices with their start and end apart: 3, of which 2 were waited for; matrix products, arithmetic and copies ran while one was open for 4% of the time, Pallas kernels for 0%

profile of v1, /device:TPU:1, one launch (start us, length us, event | category | flops | bytes accessed | tf_op | source)
XLA Modules:
  0.0 140.5 jit_solution(10042441039687070057)
XLA Ops:
  6.5 0.0 copy-start
  6.5 0.0 copy-start.1
  6.5 0.0 reduce-scatter.2.cloned.1.call-start
  6.5 0.7 copy-done
  7.2 0.1 reshape.75
  7.4 15.8 %all_to_all.15 = bf16[16,2,384]{2,1,0:T(2,128)(2,1)S(1)} all-to-all(bf16[16,2,384]{2,1,0:T(2,128)(2,1)S(1)} %reshape.75), channel_id=1, replica_groups=mesh['wide'=16,'col'=16] {'col'}, dimensions={0} | all-to-all | bytes 49152 | tf_op jit(solution)/shard_map/all_to_all | solution.py:12
  23.2 0.1 reshape.76
  23.3 6.5 %fusion.15 = f32[32,12288]{1,0:T(8,128)} fusion(bf16[32,384]{0,1:T(8,128)(2,1)S(1)} %bitcast.36, bf16[384,12288]{1,0:T(8,128)(2,1)} %param.4), kind=kOutput, calls=%fused_computation.36 | convolution fusion | flops 301989888 | bytes 11034624 | tf_op jit(solution)/shard_map/dot_general | solution.py:25
  29.8 0.0 reduce-scatter.2.cloned.1.call-update
  29.8 0.0 copy-done.1
  29.9 1.7 %reduce-window.6 = s32[16,6,128]{2,0,1:T(8,128)S(1)} reduce-window(s32[16,6,128]{2,0,1:T(8,128)S(1)} %fusion.11, s32[]{:T(128)} %constant.48.clone.1), window={size=1x1x128 pad=0_0x0_0x127_0}, to_apply=%region_1.2 | reduce-window | flops 1560576 | bytes 98308 | tf_op jit(solution)/shard_map/reduce-window
  31.6 0.3 slice_reduce_fusion
  31.9 0.1 fusion.8
  32.0 0.7 select_reduce_fusion
  32.7 0.7 convert_element_type.40
  33.4 10.3 %all-to-all-start.2 = ((f32[1,16,16]{2,0,1:T(1,128)}), f32[1,16,16]{2,0,1:T(1,128)S(1)}, u32[]{:S(2)}, u32[]{:S(2)}) async-start(f32[1,16,16]{2,0,1:T(1,128)} %convert_element_type.40), calls=%async_computation.3 | async-start | bytes 16384 | tf_op jit(solution)/shard_map/all_to_all | solution.py:48
  43.7 68.2 %reduce-scatter.2.cloned.1.call-done = f32[32,768]{1,0:T(8,128)} async-done(((f32[32,12288]{1,0:T(8,128)}), f32[32,768]{1,0:T(8,128)}) %reduce-scatter.2.cloned.1.call-update) | async-done | bytes 98320 | tf_op jit(solution)/shard_map/reduce_scatter | solution.py:27
  111.9 1.9 %fusion.1 = f32[32,256]{0,1:T(8,128)S(1)} fusion(f32[32,768]{1,0:T(8,128)} %reduce-scatter.2.cloned.1.call-done, s32[768]{0:T(1024)S(1)} %multiply_add_fusion, pred[768]{0:T(1024)(128)(4,1)S(1)} %get-tuple-element.6), kind=kOutput, calls=%fused_computation.5 | convolution fusion | flops 75890688 | bytes 134912 | tf_op jit(solution)/shard_map/dot_general | solution.py:40
  113.8 0.7 reshape.77
  114.5 0.0 all-to-all-done.2
  114.5 6.1 %all-to-all-start.1 = ((f32[16,1,512]{2,1,0:T(1,128)}), f32[16,1,512]{2,1,0:T(1,128)S(1)}, u32[]{:S(2)}, u32[]{:S(2)}) async-start(f32[16,1,512]{2,1,0:T(1,128)} %reshape.77), calls=%async_computation.2 | async-start | bytes 65536 | tf_op jit(solution)/shard_map/all_to_all | solution.py:47
  120.7 0.1 convert_element_type.42
  120.8 9.6 %all-to-all-done.1 = f32[16,1,512]{2,1,0:T(1,128)S(1)} async-done(((f32[16,1,512]{2,1,0:T(1,128)}), f32[16,1,512]{2,1,0:T(1,128)S(1)}, u32[]{:S(2)}, u32[]{:S(2)}) %all-to-all-start.1) | async-done | bytes 32800 | tf_op jit(solution)/shard_map/all_to_all | solution.py:47
  130.4 0.5 broadcast.62
  130.9 0.7 reduce.6
  131.6 0.1 reshape.78
  131.7 2.0 %convolution_add_fusion = f32[32,768]{1,0:T(8,128)} fusion(f32[32,256]{0,1:T(8,128)S(1)} %bitcast.37, s32[256]{0:T(256)S(1)} %convert_element_type.42, f32[32,768]{1,0:T(8,128)} %reduce-scatter.2.cloned.1.call-done, f32[768]{0:T(1024)S(1)} %get-tuple-element.5), kind=kOutput, calls=%fused_computation | convolution fusion | flops 75743232 | bytes 233472 | tf_op jit(solution)/shard_map/dot_general | solution.py:54
  (8 shorter events, 0.1 us)
Async XLA Ops:
  6.5 0.7 copy-start
  6.5 23.3 %copy-start.1 = (s32[768]{0:T(1024)S(1)}, s32[768]{0:T(1024)}, u32[]{:S(2)}) copy-start(s32[768]{0:T(1024)} %param.5) | copy-start | bytes 9220
  6.5 105.3 %reduce-scatter.2.cloned.1.call-start = ((), (), s32[]{:S(2)}) async-start(), calls=%async_computation.4 | async-start | bytes 1671168 | tf_op jit(solution)/shard_map/reduce_scatter | solution.py:27
  33.4 81.2 %all-to-all-start.2 = ((f32[1,16,16]{2,0,1:T(1,128)}), f32[1,16,16]{2,0,1:T(1,128)S(1)}, u32[]{:S(2)}, u32[]{:S(2)}) async-start(f32[1,16,16]{2,0,1:T(1,128)} %convert_element_type.40), calls=%async_computation.3 | async-start | bytes 16384 | tf_op jit(solution)/shard_map/all_to_all | solution.py:48
  114.5 15.9 %all-to-all-start.1 = ((f32[16,1,512]{2,1,0:T(1,128)}), f32[16,1,512]{2,1,0:T(1,128)S(1)}, u32[]{:S(2)}, u32[]{:S(2)}) async-start(f32[16,1,512]{2,1,0:T(1,128)} %reshape.77), calls=%async_computation.2 | async-start | bytes 65536 | tf_op jit(solution)/shard_map/all_to_all | solution.py:47
Sparse Core Ops, SparseCore 0:
  29.9 81.8 reduce-scatter.1
